TPU v7x, 32 devices: a whole 2x2x4 slice. The times are simulated.
32 devices in a mesh: grp: 2 (over x), row: 16 (over z, y, core).
Axes of the slice: x: 2, y: 2, z: 4, core: 2. Of those that a mesh axis runs over, the one named last changes fastest.
Arguments:
- coupling_features: bfloat16 [1024, 512, 128], P(('grp', 'row')), parts along dimension 0, may hold values from -6 to 6
- aligned_features: bfloat16 [256, 512, 256], P(('grp', 'row')), parts along dimension 0, may hold values from -6 to 6
- aligned_entry_flags: int32 [256, 512], P('grp'), parts along dimension 0, may hold values 0 or 1
- amino_real_flags: int32 [1024], P('grp'), parts along dimension 0, may hold values from 0 to 1, as said below
- coupling_offset_matrix: bfloat16 [128, 8], replicated, may hold values from -3.5 to 3.5
- lookup_matrices: bfloat16 [256, 1024], replicated, may hold values from -0.75 to 0.75
- aligned_final_matrix: bfloat16 [256, 256], replicated, may hold values from -0.375 to 0.375
- product_factor_matrices: bfloat16 [256, 64], replicated, may hold values from -0.375 to 0.375
- product_final_matrix: bfloat16 [1024, 128], replicated, may hold values from -1 to 1
- trio_factor_matrices: bfloat16 [128, 640], replicated, may hold values from -0.5 to 0.5
- trio_final_matrix: bfloat16 [128, 128], replicated, may hold values from -0.5 to 0.5
- feedforward_expand: bfloat16 [128, 512], replicated, may hold values from -0.5 to 0.5
- feedforward_shrink: bfloat16 [512, 128], replicated, may hold values from -0.25 to 0.25
Outputs:
- msa_out: bfloat16 [256, 512, 256], P(('grp', 'row')), parts along dimension 0
- coupling_refreshed: bfloat16 [1024, 512, 128], P(('grp', 'row')), parts along dimension 0
There are 2 independent parts, one for each index of `grp`. A program takes and returns all parts, laid end to end along the dimension named above; an argument that names none is the same for every part. Nothing has to cross between parts.
Inputs may be any that keep to these rules, and one draw needn't show every extreme that they name: `amino_real_flags`: 1 on a prefix of at least 256 residues and 0 on the rest, which is never empty.
All inputs are finite; a program needn't handle non-finite values.
Results may differ from a plain program's by a relative error of at most 0.008.
The roundings to bfloat16 on the way count: a program that leaves them out, or rounds other values in their place, can miss the bound.
Values may be sent and summed in bfloat16 or wider, within the bound.
No kernel may reach another device: no remote copies, remote signals or barrier semaphores. Data moves between devices by JAX's collectives and lax.ppermute only.
A program may use at most 192 MiB of HBM per device.

v0:
```python
import functools

import jax
import jax.numpy as jnp
from jax import lax
from jax.experimental import pallas as pl
from jax.experimental.pallas import tpu as pltpu
from jax.sharding import PartitionSpec as P


EPSILON = 1e-05
F32 = jnp.float32
BF16 = jnp.bfloat16
LANES = 128
HEAD_UNROLL = 4
TAIL_UNROLL = 2
TAIL_ROWS = 8


def norm(values, axis=-1):
    centered = values - jnp.mean(values, axis=axis, keepdims=True)
    variance = jnp.mean(centered * centered, axis=axis, keepdims=True)
    return centered * lax.rsqrt(variance + EPSILON)


def dot(a, b, ca=1, cb=0):
    return lax.dot_general(a, b, (((ca,), (cb,)), ((), ())), preferred_element_type=F32)


def divisor(total, limit):
    best = min(total, limit)
    while total % best:
        best -= 1
    return best


def put_rows(scr, first, rows, values):
    for n in range(scr.shape[0]):
        scr[n, pl.ds(first, values.shape[0], stride=rows), :] = values[:, n * LANES : (n + 1) * LANES]


def get_rows(scr, first, rows):
    count = scr.shape[1] // rows
    return jnp.concatenate([scr[n, pl.ds(first, count, stride=rows), :] for n in range(scr.shape[0])], axis=1)


def full(shape):
    return pl.BlockSpec(shape, lambda *_: (0,) * len(shape))


def bias_kernel(x_ref, w_ref, o_ref, scr):
    rows = x_ref.shape[0]
    heads = w_ref.shape[0]

    def row(i, carry):
        xn = norm(x_ref[i].astype(F32)).astype(BF16)
        put_rows(scr, i, rows, dot(w_ref[...], xn, 1, 1))
        return carry

    lax.fori_loop(0, rows, row, 0, unroll=HEAD_UNROLL)
    for n in range(scr.shape[0]):
        o_ref[:, :, n * LANES : (n + 1) * LANES] = scr[n].astype(BF16).reshape(heads, rows, LANES)


def pair_bias(x, w):
    owned, res, cz = x.shape
    rows = divisor(owned, 16)
    heads = w.shape[0]
    return pl.pallas_call(
        bias_kernel,
        grid=(owned // rows,),
        in_specs=[pl.BlockSpec((rows, res, cz), lambda g: (g, 0, 0)), full(w.shape)],
        out_specs=pl.BlockSpec((heads, rows, res), lambda g: (0, g, 0)),
        out_shape=jax.ShapeDtypeStruct((heads, owned, res), BF16),
        scratch_shapes=[pltpu.VMEM((res // LANES, heads * rows, LANES), F32)],
        name="pair_bias",
    )(x, w)


def head_kernel(x_ref, vi_ref, vj_ref, w_ref, tri_ref, scr):
    rows, _, cz = x_ref.shape

    def row(i, carry):
        xn = norm(x_ref[i].astype(F32)).astype(BF16)
        both = dot(w_ref[...], xn, 1, 1)
        valid = vj_ref[...] * vi_ref[0, 0, i]
        put_rows(scr, i, rows, jax.nn.sigmoid(both[0:cz]) * both[cz : 2 * cz] * valid)
        return carry

    lax.fori_loop(0, rows, row, 0, unroll=HEAD_UNROLL)
    for n in range(scr.shape[0]):
        tri_ref[:, :, n * LANES : (n + 1) * LANES] = scr[n].astype(BF16).reshape(cz, rows, LANES)


def pair_head(x, my_valid, valid, w, part=0, parts=1):
    owned, res, cz = x.shape
    owned = owned // parts
    rows = divisor(owned, 16)
    steps = owned // rows
    return pl.pallas_call(
        head_kernel,
        grid=(steps,),
        in_specs=[
            pl.BlockSpec((rows, res, cz), lambda g: (g + part * steps, 0, 0)),
            pl.BlockSpec((1, 1, rows), lambda g: (g + part * steps, 0, 0), memory_space=pltpu.SMEM),
            full((1, res)),
            full(w.shape),
        ],
        out_specs=pl.BlockSpec((cz, rows, res), lambda g: (0, g, 0)),
        out_shape=jax.ShapeDtypeStruct((cz, owned, res), BF16),
        scratch_shapes=[pltpu.VMEM((res // LANES, cz * rows, LANES), F32)],
        name="pair_head",
    )(x, my_valid.reshape(-1, 1, rows), valid.reshape(1, res), w)


def msa_kernel(width, chunk, order, x_ref, valid_ref, bias_ref, w_ref, wf_ref, wp_ref, o_ref, l_ref, r_ref, q_s, k_s, v_s, att):
    res, feat = x_ref.shape[1:]
    half = feat // 2
    per_half = half // width
    x = x_ref[0].astype(F32)
    xn = norm(x).astype(BF16)
    q_s[...] = (dot(xn, w_ref[:, 0:feat]) * width ** (-0.5)).astype(BF16)
    k_s[...] = dot(xn, w_ref[:, feat : 2 * feat]).astype(BF16)
    v_s[...] = dot(xn, w_ref[:, 2 * feat : 3 * feat]).astype(BF16)
    valid = valid_ref[0]
    lane = lax.broadcasted_iota(jnp.int32, (1, feat), 1) // width
    lane_half = lax.broadcasted_iota(jnp.int32, (1, half), 1) // width

    def heads(step, carry):
        for side in (0, 1):
            mine = lane == step + side * per_half
            mine_half = lane_half == step
            v = jnp.where(mine, v_s[...], jnp.ones((), BF16))
            for c in range(res // chunk):
                span = slice(c * chunk, (c + 1) * chunk)
                q = jnp.where(mine, q_s[span], jnp.zeros((), BF16))
                lines = bias_ref.shape[2]
                owners = order[c * chunk // lines : (c + 1) * chunk // lines]
                bias = jnp.concatenate([bias_ref[g, step + side * per_half] for g in owners], axis=0)
                s = dot(q, k_s[...], 1, 1) + bias.astype(F32)
                s = jnp.where(valid > 0, s, -1000000000.0)
                p = jnp.exp(s - jnp.max(s, axis=1, keepdims=True)).astype(BF16)
                out = dot(p, v)
                mixed = out[:, side * half : (side + 1) * half] / out[:, (1 - side) * half : (2 - side) * half]
                cols = slice(side * half, (side + 1) * half)
                att[span, cols] = jnp.where(mine_half, mixed, att[span, cols])
        return carry

    lax.fori_loop(0, per_half, heads, 0)
    gate = jax.nn.sigmoid(dot(xn, w_ref[:, 3 * feat : 4 * feat]))
    mixed = (att[...] * gate).astype(BF16)
    new = x + dot(mixed, wf_ref[...])
    o_ref[0] = new.astype(BF16)
    factors = dot(wp_ref[...], norm(new).astype(BF16), 1, 1) * valid
    outer = l_ref.shape[1]
    l_ref[0] = factors[0:outer].astype(BF16)
    r_ref[0] = factors[outer : 2 * outer].astype(BF16)


def msa_block(x, valid, bias, order, w, wf, wp, width):
    seqs, res, feat = x.shape
    outer = wp.shape[0] // 2
    return pl.pallas_call(
        functools.partial(msa_kernel, width, divisor(res, 256), order),
        grid=(seqs,),
        in_specs=[
            pl.BlockSpec((1, res, feat), lambda s: (s, 0, 0)),
            pl.BlockSpec((1, 1, res), lambda s: (s, 0, 0)),
            full(bias.shape),
            full(w.shape),
            full(wf.shape),
            full(wp.shape),
        ],
        out_specs=[
            pl.BlockSpec((1, res, feat), lambda s: (s, 0, 0)),
            pl.BlockSpec((1, outer, res), lambda s: (s, 0, 0)),
            pl.BlockSpec((1, outer, res), lambda s: (s, 0, 0)),
        ],
        out_shape=[
            jax.ShapeDtypeStruct((seqs, res, feat), BF16),
            jax.ShapeDtypeStruct((seqs, outer, res), BF16),
            jax.ShapeDtypeStruct((seqs, outer, res), BF16),
        ],
        scratch_shapes=[pltpu.VMEM((res, feat), BF16)] * 3 + [pltpu.VMEM((res, feat), F32)],
        name="msa_block",
    )(x, valid.reshape(seqs, 1, res), bias, w, wf, wp)


def tri_kernel(l_ref, *refs):
    groups, chans, owned, res = l_ref.shape
    o_ref = refs[-1]
    for c in range(chans):
        a = l_ref[:, c].reshape(groups * owned, res)
        for n, r_ref in enumerate(refs[:-1]):
            count = groups * r_ref.shape[2]
            part = dot(a, r_ref[:, c].reshape(count, res), 1, 1).astype(BF16)
            o_ref[:, c, :, n * count : (n + 1) * count] = part.reshape(groups, owned, count)


def tri_sums(left, rights):
    groups, chans, owned, res = left.shape
    step = divisor(chans, 4)

    def spec(rows, cols):
        return pl.BlockSpec((groups, step, rows, cols), lambda c: (0, c, 0, 0))

    cols = groups * sum(r.shape[2] for r in rights)
    return pl.pallas_call(
        tri_kernel,
        grid=(chans // step,),
        in_specs=[spec(owned, res)] + [spec(r.shape[2], res) for r in rights],
        out_specs=spec(owned, cols),
        out_shape=jax.ShapeDtypeStruct((groups, chans, owned, cols), BF16),
        name="tri_sums",
    )(left, *rights)


def opm_kernel(l_ref, r_ref, w_ref, vt_ref, vi_ref, o_ref, mix, right):
    rows, seqs, outer = l_ref.shape
    owners, inner, local, _ = r_ref.shape
    res, cz = o_ref.shape[1:]
    depth = inner * local

    @pl.when(pl.program_id(0) == 0)
    def _():
        for g in range(owners):
            right[:, g * depth : (g + 1) * depth] = r_ref[g, :, :, 0:res].reshape(depth, res).T

    many = max(16 // local, 1)
    for first in range(0, rows, 2):
        pair = min(2, rows - first)
        both = l_ref[first : first + pair].reshape(pair * seqs, outer)
        for d in range(0, inner, many):
            made = [dot(both, w_ref[:, (d + m) * cz : (d + m + 1) * cz]) for m in range(many)]
            for n in range(pair):
                for g in range(owners):
                    at = n * seqs + g * local
                    lines = jnp.concatenate([t[at : at + local] for t in made], axis=0).astype(BF16)
                    to = g * depth + d * local
                    mix[to : to + many * local, n * cz : (n + 1) * cz] = lines
        total = dot(right[...], mix[:, 0 : pair * cz])
        for n in range(pair):
            mine = jnp.broadcast_to(vi_ref[:, first + n : first + n + 1], (seqs, cz)).astype(BF16)
            tally = jnp.maximum(dot(vt_ref[...], mine), 1.0)
            o_ref[first + n] = total[:, n * cz : (n + 1) * cz] / tally


def opm_block(left, right, w, valid_t, mine):
    owned, seqs, outer = left.shape
    _, inner, _, _ = right.shape
    res = valid_t.shape[0]
    cz = w.shape[1] // inner
    rows = divisor(owned, 8)
    pair = pl.BlockSpec((rows, res, cz), lambda g: (g, 0, 0))
    return pl.pallas_call(
        opm_kernel,
        grid=(owned // rows,),
        in_specs=[
            pl.BlockSpec((rows, seqs, outer), lambda g: (g, 0, 0)),
            full(right.shape),
            full(w.shape),
            full(valid_t.shape),
            pl.BlockSpec((None, seqs, rows), lambda g: (g, 0, 0)),
        ],
        out_specs=pair,
        out_shape=jax.ShapeDtypeStruct((owned, res, cz), F32),
        scratch_shapes=[pltpu.VMEM((seqs * inner, 2 * cz), BF16), pltpu.VMEM((res, seqs * inner), BF16)],
        name="opm_block",
    )(left, right, w, valid_t, mine.reshape(seqs, owned // rows, rows).transpose(1, 0, 2))


def tail_kernel(table_ref, x_ref, tri_ref, opm_ref, wg_ref, wt_ref, w1_ref, w2_ref, *refs):
    o_ref, scr = refs[-2:]
    rows, groups, lines, cz = x_ref.shape
    cols = groups * lines
    many = divisor(rows, TAIL_ROWS)
    for n in range(scr.shape[0]):
        part = tri_ref[:, :, n * LANES : (n + 1) * LANES]
        scr[n] = part.astype(F32).reshape(scr.shape[1:])

    def block(b, carry):
        i = b * many
        x = x_ref[pl.ds(i, many)].reshape(many * cols, cz).astype(F32)
        gate = jax.nn.sigmoid(dot(norm(x).astype(BF16), wg_ref[...]))
        tri = [dot(norm(get_rows(scr, i + m, rows), 0).astype(BF16), wt_ref[...], 0, 0) for m in range(many)]
        one = x + gate * jnp.concatenate(tri, axis=0)
        hidden = jnp.maximum(dot(norm(one).astype(BF16), w1_ref[...]), 0.0).astype(BF16)
        out = one + dot(hidden, w2_ref[...]) + opm_ref[pl.ds(i, many)].reshape(many * cols, cz)
        o_ref[pl.ds(i, many)] = out.astype(o_ref.dtype).reshape(many, groups, lines, cz)
        return carry

    lax.fori_loop(0, rows // many, block, 0, unroll=TAIL_UNROLL)


def pair_tail(table, parts, x, tri, opm, weights, earlier=None):
    owned, res, cz = x.shape
    ring = res // owned
    rows = divisor(owned, 16)
    lines = owned // parts
    span = ring // 2 * lines
    view = (owned, ring, parts, lines, cz)
    pair = pl.BlockSpec((rows, ring // 2, None, lines, cz), lambda q, g, t: (g, t[0, q], t[1, q], 0, 0))
    in_specs = [pair, pl.BlockSpec((cz, rows, span), lambda q, g, t: (0, g, q)), pair]
    in_specs += [full(w.shape) for w in weights]
    args = [table, x.reshape(view), tri, opm.reshape(view), *weights]
    aliases = {}
    if earlier is not None:
        aliases = {len(args): 0}
        in_specs.append(pl.BlockSpec(memory_space=pl.ANY))
        args.append(earlier.reshape(view))
    return pl.pallas_call(
        tail_kernel,
        grid_spec=pltpu.PrefetchScalarGridSpec(
            num_scalar_prefetch=1,
            grid=(tri.shape[2] // span, owned // rows),
            in_specs=in_specs,
            out_specs=pair,
            scratch_shapes=[pltpu.VMEM((max(span // LANES, 1), cz * rows, min(span, LANES)), F32)],
        ),
        out_shape=jax.ShapeDtypeStruct(view, BF16),
        input_output_aliases=aliases,
        name="pair_tail",
    )(*args).reshape(owned, res, cz)


def body(
    ring,
    coupling_features,
    aligned_features,
    aligned_entry_flags,
    amino_real_flags,
    coupling_offset_matrix,
    lookup_matrices,
    aligned_final_matrix,
    product_factor_matrices,
    product_final_matrix,
    trio_factor_matrices,
    trio_final_matrix,
    feedforward_expand,
    feedforward_shrink,
):
    owned, res, cz = coupling_features.shape
    seqs, _, feat = aligned_features.shape
    width = feat // coupling_offset_matrix.shape[1]
    outer = product_factor_matrices.shape[1] // 2
    place = lax.axis_index("row")
    near = ring // 2
    halves = [list(range(near)), list(range(near, ring))]
    swap = [(r, (r + near) % ring) for r in range(ring)]

    residue = amino_real_flags.astype(F32)
    entry = aligned_entry_flags.astype(F32) * residue[None, :]
    my_residue = lax.dynamic_slice_in_dim(residue, place * owned, owned, 0)
    my_entry = lax.dynamic_slice_in_dim(entry, place * seqs, seqs, 0)
    trio = trio_factor_matrices.T

    parts = 2 if owned % 32 == 0 else 1
    half = (place // near).astype(jnp.int32)

    def spread(values):
        values = values.reshape(near, cz // near, values.shape[1], values.shape[-1])
        return lax.all_to_all(values, "row", 0, 0, tiled=True, axis_index_groups=halves)

    bias = pair_bias(coupling_features, coupling_offset_matrix.T)
    made = []
    for part in range(parts):
        made.append(
            pair_head(coupling_features, my_residue, residue, trio[2 * cz : 4 * cz], part, parts)
        )

    planes = 4 if ring % 4 == 0 else 1
    members = ring // planes
    plane = place // members
    within = [[m + members * z for m in range(members)] for z in range(planes)]
    order = [m * planes + z for z in range(planes) for m in range(members)]

    def across(values):
        got = [values[0]]
        for k in range(1, planes):
            got.append(lax.ppermute(values[k], "row", [(r, r ^ (k * members)) for r in range(ring)]))
        got = jnp.stack(got)
        return jnp.stack([lax.dynamic_index_in_dim(got, plane ^ z, 0, keepdims=False) for z in range(planes)])

    def gather(values):
        values = lax.all_gather(values, "row", axis=0, axis_index_groups=within)
        return values.reshape((ring,) + values.shape[2:])

    bias = across([bias] * planes)
    right_own, right_oth = [], []
    for part in range(parts):
        right = made[part]
        right_own.append(spread(right))
        right_oth.append(lax.ppermute(right_own[part], "row", swap))
    left = pair_head(coupling_features, my_residue, residue, trio[0 : 2 * cz])
    left, bias = lax.optimization_barrier((left, bias))
    left_own = spread(left)
    bias_all = gather(bias)

    msa_out, left_opm, right_opm = msa_block(
        aligned_features,
        my_entry,
        bias_all,
        order,
        lookup_matrices,
        aligned_final_matrix,
        product_factor_matrices.T,
        width,
    )

    def collect(sums):
        back = lax.all_to_all(sums, "row", 0, 0, tiled=True, axis_index_groups=halves)
        return back.reshape(cz, owned, sums.shape[-1])

    spot = res // planes
    both = []
    for k in range(planes):
        lines = lax.dynamic_slice_in_dim(left_opm, (plane ^ k) * spot, spot, 2)
        both.append(jnp.concatenate([right_opm, lines], axis=2).transpose(1, 0, 2))
    both = gather(across(both))
    left_res = lax.dynamic_slice_in_dim(both, res + (place % members) * owned, owned, 3)
    left_res = left_res.transpose(3, 0, 2, 1).reshape(owned, ring * seqs, outer)
    entry_order = entry.reshape(planes, members, seqs, res).transpose(1, 0, 2, 3).reshape(ring * seqs, res)
    mine = lax.dynamic_slice_in_dim(entry_order, place * owned, owned, 1)
    opm = opm_block(left_res, both, product_final_matrix.reshape(outer, outer * cz), entry_order.T.astype(BF16), mine)

    sums = tri_sums(left_own, right_own + right_oth[:-1])
    tri_near = collect(sums)
    sums = tri_sums(left_own, right_oth[-1:])
    tri_last = collect(sums)
    weights = (trio_factor_matrices[:, 4 * cz : 5 * cz], trio_final_matrix, feedforward_expand, feedforward_shrink)
    table = jnp.array([[0] * parts + [1] * parts, list(range(parts)) * 2], jnp.int32)
    table = table.at[0].set(table[0] ^ half)
    pair = pair_tail(table[:, :-1], parts, coupling_features, tri_near, opm, weights)
    pair = pair_tail(table[:, -1:], parts, coupling_features, tri_last, opm, weights, earlier=pair)
    return (msa_out, pair)


def solution(mesh):


    return jax.shard_map(
        functools.partial(body, mesh.shape["row"]),
        mesh=mesh,
        in_specs=(
            P(("grp", "row"), None, None),
            P(("grp", "row"), None, None),
            P("grp", None),
            P("grp"),
            P(),
            P(),
            P(),
            P(),
            P(),
            P(),
            P(),
            P(),
            P(),
        ),
        out_specs=(P(("grp", "row"), None, None), P(("grp", "row"), None, None)),
        check_vma=False,
    )
```

profile of v0, /device:TPU:13, one launch (start us, length us, event | category | flops | bytes accessed | tf_op | source)
XLA Modules:
  0.0 462.7 jit_solution(7169999148098138659)
XLA Ops:
  10.3 8.6 %pair_head.5 = bf16[128,16,512]{2,1,0:T(8,128)(2,1)} custom-call(bf16[32,512,128]{2,1,0:T(8,128)(2,1)} %x_ref.9, f32[2,1,16]{2,1,0:T(1,128)} %bitcast.71, f32[1,512]{1,0:T(1,128)} %bitcast.67, bf16[256,128]{1,0:T(8,128)(2,1)} %get-tuple-element.40.w_ref), custom_call_target="tpu_custom_call" | custom-call | tf_op jit(solution)/shard_map/pair_head/pallas_call | solution.py:100
  18.9 4.5 all-to-all-start.3
  23.4 8.6 %pair_head.4 = bf16[128,16,512]{2,1,0:T(8,128)(2,1)} custom-call(bf16[32,512,128]{2,1,0:T(8,128)(2,1)} %x_ref.9, f32[2,1,16]{2,1,0:T(1,128)} %bitcast.72, f32[1,512]{1,0:T(1,128)} %bitcast.68, bf16[256,128]{1,0:T(8,128)(2,1)} %get-tuple-element.40.w_ref), custom_call_target="tpu_custom_call" | custom-call | tf_op jit(solution)/shard_map/pair_head/pallas_call | solution.py:100
  32.0 15.1 %all-to-all-done.3.refs_0_ = bf16[8,16,16,512]{3,2,1,0:T(8,128)(2,1)S(1)} async-done(((bf16[8,16,16,512]{3,2,1,0:T(8,128)(2,1)}), bf16[8,16,16,512]{3,2,1,0:T(8,128)(2,1)S(1)}, u32[]{:S(2)}, u32[]{:S(2)}) %all-to-all-start.3) | async-done | bytes 2097184 | tf_op jit(solution)/shard_map/all_to_all | solution.py:362
  47.1 6.3 %all-to-all-start.1 = ((bf16[8,16,16,512]{3,2,1,0:T(8,128)(2,1)}), bf16[8,16,16,512]{3,2,1,0:T(8,128)(2,1)}, u32[]{:S(2)}, u32[]{:S(2)}) async-start(bf16[8,16,16,512]{3,2,1,0:T(8,128)(2,1)} %bitcast.50), calls=%async_computation.1 | async-start | bytes 4194304 | tf_op jit(solution)/shard_map/all_to_all | solution.py:362
  53.4 8.5 %pair_bias.1 = bf16[8,32,512]{2,1,0:T(8,128)(2,1)} custom-call(bf16[32,512,128]{2,1,0:T(8,128)(2,1)} %x_ref.9, bf16[8,128]{1,0:T(8,128)(2,1)} %bitcast.75), custom_call_target="tpu_custom_call" | custom-call | tf_op jit(solution)/shard_map/pair_bias/pallas_call | solution.py:69
  61.9 1.4 collective-permute-start.2
  65.4 14.3 %pair_head.3 = bf16[128,32,512]{2,1,0:T(8,128)(2,1)} custom-call(bf16[32,512,128]{2,1,0:T(8,128)(2,1)} %x_ref.9, f32[2,1,16]{2,1,0:T(1,128)} %bitcast.73, f32[1,512]{1,0:T(1,128)} %bitcast.69, bf16[256,128]{1,0:T(8,128)(2,1)} %get-tuple-element.41.w_ref), custom_call_target="tpu_custom_call" | custom-call | tf_op jit(solution)/shard_map/pair_head/pallas_call | solution.py:100
  79.7 10.6 %collective-permute-done.1 = bf16[8,32,512]{2,1,0:T(8,128)(2,1)S(1)} collective-permute-done((bf16[8,32,512]{2,1,0:T(8,128)(2,1)}, bf16[8,32,512]{2,1,0:T(8,128)(2,1)S(1)}, u32[]{:S(2)}, u32[]{:S(2)}) %collective-permute-start.1) | collective-permute-done | bytes 262176 | tf_op jit(solution)/shard_map/ppermute | solution.py:380
  90.3 3.6 collective-permute-done
  95.3 6.7 %all-to-all-start = ((bf16[8,16,32,512]{3,2,1,0:T(8,128)(2,1)}), bf16[8,16,32,512]{3,2,1,0:T(8,128)(2,1)}, u32[]{:S(2)}, u32[]{:S(2)}) async-start(bf16[8,16,32,512]{3,2,1,0:T(8,128)(2,1)} %bitcast.47), calls=%async_computation | async-start | bytes 8388608 | tf_op jit(solution)/shard_map/all_to_all | solution.py:362
  102.0 2.4 collective-permute-start.7
  105.1 67.8 %all-gather.5.cloned.1.call-done.bias_ref = bf16[16,8,32,512]{3,2,1,0:T(8,128)(2,1)} async-done(((bf16[4,8,32,512]{3,2,1,0:T(8,128)(2,1)}), bf16[16,8,32,512]{3,2,1,0:T(8,128)(2,1)}) %all-gather.5.cloned.1.call-update) | async-done | bytes 4194320 | tf_op jit(solution)/shard_map/all_gather | solution.py:385
  172.8 50.2 %msa_block.1 = (bf16[8,512,256]{2,1,0:T(8,128)(2,1)}, bf16[8,32,512]{2,1,0:T(8,128)(2,1)}, bf16[8,32,512]{2,1,0:T(8,128)(2,1)}) custom-call(bf16[8,512,256]{2,1,0:T(8,128)(2,1)} %x_ref.7, f32[8,1,512]{2,1,0:T(1,128)} %reshape.88.valid_ref, bf16[16,8,32,512]{3,2,1,0:T(8,128)(2,1)} %all-gather.5.cloned.1.call-done.bias_ref, bf16[256,1024]{1,0:T(8,128)(2,1)} %w_ref.1, ...), custom_call_target="tpu_custom_call" | custom-call | tf_op jit(solution)/shard_map/msa_block/pallas_call | solution.py:163
  225.2 2.4 collective-permute-start.5
  227.8 10.8 %collective-permute-done.4 = bf16[32,8,640]{2,0,1:T(8,128)(2,1)S(1)} collective-permute-done((bf16[32,8,640]{2,0,1:T(8,128)(2,1)S(1)}, bf16[32,8,640]{2,0,1:T(8,128)(2,1)S(1)}, u32[]{:S(2)}, u32[]{:S(2)}) %collective-permute-start.4) | collective-permute-done | bytes 327712 | tf_op jit(solution)/shard_map/ppermute | solution.py:380
  238.6 3.7 collective-permute-done.5
  242.3 13.9 %collective-permute-done.6 = bf16[32,8,640]{2,0,1:T(8,128)(2,1)S(1)} collective-permute-done((bf16[32,8,640]{2,0,1:T(8,128)(2,1)S(1)}, bf16[32,8,640]{2,0,1:T(8,128)(2,1)S(1)}, u32[]{:S(2)}, u32[]{:S(2)}) %collective-permute-start.6) | collective-permute-done | bytes 327712 | tf_op jit(solution)/shard_map/ppermute | solution.py:380
  256.8 1.5 copy.66
  258.3 7.7 %tri_sums.3 = bf16[8,16,32,384]{3,2,1,0:T(8,128)(2,1)} custom-call(bf16[8,16,32,512]{3,2,1,0:T(8,128)(2,1)} %all-to-all-done.l_ref, bf16[8,16,16,512]{3,2,1,0:T(8,128)(2,1)} %copy-done.1, bf16[8,16,16,512]{3,2,1,0:T(8,128)(2,1)} %all-to-all-done.1.refs_1_, bf16[8,16,16,512]{3,2,1,0:T(8,128)(2,1)} %collective-permute-done.7.refs_2_), custom_call_target="tpu_custom_call" | custom-call | tf_op jit(solution)/shard_map/tri_sums/pallas_call | solution.py:208
  266.0 5.3 %all-to-all-start.4 = ((bf16[8,16,32,384]{3,2,1,0:T(8,128)(2,1)}), bf16[8,16,32,384]{3,2,1,0:T(8,128)(2,1)S(1)}, u32[]{:S(2)}, u32[]{:S(2)}) async-start(bf16[8,16,32,384]{3,2,1,0:T(8,128)(2,1)} %tri_sums.3), calls=%async_computation.4 | async-start | bytes 6291456 | tf_op jit(solution)/shard_map/all_to_all | solution.py:411
  271.3 3.3 collective-permute-start.3
  274.6 89.9 %collective-permute-done.3.refs_0_ = bf16[8,16,16,512]{3,2,1,0:T(8,128)(2,1)} collective-permute-done((bf16[8,16,16,512]{3,2,1,0:T(8,128)(2,1)}, bf16[8,16,16,512]{3,2,1,0:T(8,128)(2,1)}, u32[]{:S(2)}, u32[]{:S(2)}) %collective-permute-start.3) | collective-permute-done | bytes 2097184 | tf_op jit(solution)/shard_map/ppermute | solution.py:393
  364.5 5.1 %tri_sums.2 = bf16[8,16,32,128]{3,2,1,0:T(8,128)(2,1)} custom-call(bf16[8,16,32,512]{3,2,1,0:T(8,128)(2,1)} %all-to-all-done.l_ref, bf16[8,16,16,512]{3,2,1,0:T(8,128)(2,1)} %collective-permute-done.3.refs_0_), custom_call_target="tpu_custom_call" | custom-call | tf_op jit(solution)/shard_map/tri_sums/pallas_call | solution.py:208
  369.7 6.1 %all-to-all-start.2 = ((bf16[8,16,32,128]{3,2,1,0:T(8,128)(2,1)}), bf16[8,16,32,128]{3,2,1,0:T(8,128)(2,1)}, u32[]{:S(2)}, u32[]{:S(2)}) async-start(bf16[8,16,32,128]{3,2,1,0:T(8,128)(2,1)} %tri_sums.2), calls=%async_computation.2 | async-start | bytes 2097152 | tf_op jit(solution)/shard_map/all_to_all | solution.py:411
  375.8 1.4 slice.38.wg_ref
  380.7 1.8 reshape.97.w_ref
  382.4 2.6 dynamic-slice_bitcast_fusion
  385.0 3.8 copy.67
  388.8 35.1 %opm_block.1 = f32[32,512,128]{2,1,0:T(8,128)} custom-call(bf16[32,128,32]{2,1,0:T(8,128)(2,1)} %bitcast.52, bf16[16,32,8,640]{3,2,1,0:T(8,128)(2,1)} %all-gather.7.cloned.1.call-done.r_ref, bf16[32,4096]{1,0:T(8,128)(2,1)} %reshape.97.w_ref, bf16[512,128]{1,0:T(8,128)(2,1)} %bitcast.59, f32[4,128,8]{2,1,0:T(8,128)} %bitcast.57), custom_call_target="tpu_custom_call" | custom-call | tf_op jit(solution)/shard_map/opm_block/pallas_call | solution.py:255
  423.8 22.4 %pair_tail.2.refs_0_ = bf16[32,16,2,16,128]{4,3,2,1,0:T(8,128)(2,1)} custom-call(s32[2,3]{1,0:T(2,128)} %bitcast.74, bf16[32,16,2,16,128]{4,3,2,1,0:T(8,128)(2,1)} %bitcast.43, bf16[128,32,384]{2,1,0:T(8,128)(2,1)} %bitcast.49, f32[32,16,2,16,128]{4,3,2,1,0:T(8,128)} %bitcast.45, bf16[128,128]{1,0:T(8,128)(2,1)} %slice.38.wg_ref, bf16[128,128]{1,0:T(8,128)(2,1)} %wt_ref.3, ...), custom_call_target="tpu_custom_call" | custom-call | tf_op jit(solution)/shard_map/pair_tail/pallas_call | solution.py:311
  446.2 9.7 %pair_tail.3 = bf16[32,16,2,16,128]{4,3,2,1,0:T(8,128)(2,1)} custom-call(s32[2,1]{1,0:T(2,128)} %slice.36.table_ref, bf16[32,16,2,16,128]{4,3,2,1,0:T(8,128)(2,1)} %bitcast.44, bf16[128,32,128]{2,1,0:T(8,128)(2,1)} %bitcast.12.tri_ref, f32[32,16,2,16,128]{4,3,2,1,0:T(8,128)} %bitcast.46, ...), custom_call_target="tpu_custom_call", output_to_operand_aliasing={{}: (8, {})} | custom-call | tf_op jit(solution)/shard_map/pair_tail/pallas_call | solution.py:311
  (60 shorter events, 13.8 us)
Async XLA Ops:
  7.9 2.5 copy-start.5
  18.9 28.2 %all-to-all-start.3 = ((bf16[8,16,16,512]{3,2,1,0:T(8,128)(2,1)}), bf16[8,16,16,512]{3,2,1,0:T(8,128)(2,1)S(1)}, u32[]{:S(2)}, u32[]{:S(2)}) async-start(bf16[8,16,16,512]{3,2,1,0:T(8,128)(2,1)} %bitcast.51), calls=%async_computation.3 | async-start | bytes 4194304 | tf_op jit(solution)/shard_map/all_to_all | solution.py:362
  47.1 54.9 %copy-start.1 = (bf16[8,16,16,512]{3,2,1,0:T(8,128)(2,1)}, bf16[8,16,16,512]{3,2,1,0:T(8,128)(2,1)S(1)}, u32[]{:S(2)}) copy-start(bf16[8,16,16,512]{3,2,1,0:T(8,128)(2,1)S(1)} %all-to-all-done.3.refs_0_) | copy-start | bytes 6291460
  47.1 48.2 %all-to-all-start.1 = ((bf16[8,16,16,512]{3,2,1,0:T(8,128)(2,1)}), bf16[8,16,16,512]{3,2,1,0:T(8,128)(2,1)}, u32[]{:S(2)}, u32[]{:S(2)}) async-start(bf16[8,16,16,512]{3,2,1,0:T(8,128)(2,1)} %bitcast.50), calls=%async_computation.1 | async-start | bytes 4194304 | tf_op jit(solution)/shard_map/all_to_all | solution.py:362
  53.4 119.5 %all-gather.5.cloned.1.call-start = ((), (), s32[]{:S(2)}) async-start(), calls=%async_computation.5 | async-start | bytes 5242880 | tf_op jit(solution)/shard_map/all_gather | solution.py:385
  61.9 17.8 %collective-permute-start.2 = (bf16[8,32,512]{2,1,0:T(8,128)(2,1)}, bf16[8,32,512]{2,1,0:T(8,128)(2,1)S(1)}, u32[]{:S(2)}, u32[]{:S(2)}) collective-permute-start(bf16[8,32,512]{2,1,0:T(8,128)(2,1)} %pair_bias.1), channel_id=1, source_target_pairs={{0,12},{1,13},{2,14},{3,15},{4,8},{5,9},{6,10},{7,11},{8,4},{9,5},... | collective-permute-start | bytes 786440 | tf_op jit(solution)/shard_map/ppermute | solution.py:380
  63.3 27.0 %collective-permute-start.1 = (bf16[8,32,512]{2,1,0:T(8,128)(2,1)}, bf16[8,32,512]{2,1,0:T(8,128)(2,1)S(1)}, u32[]{:S(2)}, u32[]{:S(2)}) collective-permute-start(bf16[8,32,512]{2,1,0:T(8,128)(2,1)} %pair_bias.1), channel_id=1, source_target_pairs={{0,8},{1,9},{2,10},{3,11},{4,12},{5,13},{6,14},{7,15},{8,0},{9,1},... | collective-permute-start | bytes 786440 | tf_op jit(solution)/shard_map/ppermute | solution.py:380
  64.2 29.7 %collective-permute-start = (bf16[8,32,512]{2,1,0:T(8,128)(2,1)}, bf16[8,32,512]{2,1,0:T(8,128)(2,1)S(1)}, u32[]{:S(2)}, u32[]{:S(2)}) collective-permute-start(bf16[8,32,512]{2,1,0:T(8,128)(2,1)} %pair_bias.1), channel_id=1, source_target_pairs={{0,4},{1,5},{2,6},{3,7},{4,0},{5,1},{6,2},{7,3},{8,12},{9,13},{10,... | collective-permute-start | bytes 786440 | tf_op jit(solution)/shard_map/ppermute | solution.py:380
  65.4 28.5 %copy-start.3 = (bf16[8,32,512]{2,1,0:T(8,128)(2,1)S(1)}, bf16[8,32,512]{2,1,0:T(8,128)(2,1)}, u32[]{:S(2)}) copy-start(bf16[8,32,512]{2,1,0:T(8,128)(2,1)} %pair_bias.1) | copy-start | bytes 786436
  95.3 9.1 %copy-start.4 = (s32[128,512]{1,0:T(8,128)S(1)}, s32[128,512]{1,0:T(8,128)}, u32[]{:S(2)}) copy-start(s32[128,512]{1,0:T(8,128)} %param.18) | copy-start | bytes 786436
  95.3 9.1 %copy-start.6 = (f32[512]{0:T(512)S(1)}, f32[512]{0:T(512)}, u32[]{:S(2)}) copy-start(f32[512]{0:T(512)} %copy-done.5) | copy-start | bytes 6148
  95.3 163.0 %all-to-all-start = ((bf16[8,16,32,512]{3,2,1,0:T(8,128)(2,1)}), bf16[8,16,32,512]{3,2,1,0:T(8,128)(2,1)}, u32[]{:S(2)}, u32[]{:S(2)}) async-start(bf16[8,16,32,512]{3,2,1,0:T(8,128)(2,1)} %bitcast.47), calls=%async_computation | async-start | bytes 8388608 | tf_op jit(solution)/shard_map/all_to_all | solution.py:362
  102.0 280.5 %all-gather.7.cloned.1.call-start = ((), (), s32[]{:S(2)}) async-start(), calls=%async_computation.6 | async-start | bytes 6553600 | tf_op jit(solution)/shard_map/all_gather | solution.py:385
  102.0 156.3 %collective-permute-start.7 = (bf16[8,16,16,512]{3,2,1,0:T(8,128)(2,1)S(1)}, bf16[8,16,16,512]{3,2,1,0:T(8,128)(2,1)}, u32[]{:S(2)}, u32[]{:S(2)}) collective-permute-start(bf16[8,16,16,512]{3,2,1,0:T(8,128)(2,1)S(1)} %all-to-all-done.3.refs_0_), channel_id=1, source_target_pairs={{0,8},{1,9},{2,10},{3,11},{4,12},{5,13},{6,14},{7,15},{8,0},{9,1},... | collective-permute-start | bytes 6291464 | tf_op jit(solution)/shard_map/ppermute | solution.py:393
  104.4 118.7 %copy-start.2 = (f32[128,512]{1,0:T(8,128)}, f32[128,512]{1,0:T(8,128)S(1)}, u32[]{:S(2)}) copy-start(f32[128,512]{1,0:T(8,128)S(1)} %convert_multiply_fusion) | copy-start | bytes 786436
  225.1 13.5 %collective-permute-start.4 = (bf16[32,8,640]{2,0,1:T(8,128)(2,1)S(1)}, bf16[32,8,640]{2,0,1:T(8,128)(2,1)S(1)}, u32[]{:S(2)}, u32[]{:S(2)}) collective-permute-start(bf16[32,8,640]{2,0,1:T(8,128)(2,1)S(1)} %get-tuple-element.33), channel_id=1, source_target_pairs={{0,4},{1,5},{2,6},{3,7},{4,0},{5,1},{6,2},{7,3},{8,12},{9,13},{10,... | collective-permute-start | bytes 983048 | tf_op jit(solution)/shard_map/ppermute | solution.py:380
  225.2 17.1 %collective-permute-start.5 = (bf16[32,8,640]{2,0,1:T(8,128)(2,1)S(1)}, bf16[32,8,640]{2,0,1:T(8,128)(2,1)S(1)}, u32[]{:S(2)}, u32[]{:S(2)}) collective-permute-start(bf16[32,8,640]{2,0,1:T(8,128)(2,1)S(1)} %get-tuple-element.34), channel_id=1, source_target_pairs={{0,8},{1,9},{2,10},{3,11},{4,12},{5,13},{6,14},{7,15},{8,0},{9,1},... | collective-permute-start | bytes 983048 | tf_op jit(solution)/shard_map/ppermute | solution.py:380
  227.6 28.5 %collective-permute-start.6 = (bf16[32,8,640]{2,0,1:T(8,128)(2,1)S(1)}, bf16[32,8,640]{2,0,1:T(8,128)(2,1)S(1)}, u32[]{:S(2)}, u32[]{:S(2)}) collective-permute-start(bf16[32,8,640]{2,0,1:T(8,128)(2,1)S(1)} %get-tuple-element.35), channel_id=1, source_target_pairs={{0,12},{1,13},{2,14},{3,15},{4,8},{5,9},{6,10},{7,11},{8,4},{9,5},... | collective-permute-start | bytes 983048 | tf_op jit(solution)/shard_map/ppermute | solution.py:380
  266.0 103.6 %all-to-all-start.4 = ((bf16[8,16,32,384]{3,2,1,0:T(8,128)(2,1)}), bf16[8,16,32,384]{3,2,1,0:T(8,128)(2,1)S(1)}, u32[]{:S(2)}, u32[]{:S(2)}) async-start(bf16[8,16,32,384]{3,2,1,0:T(8,128)(2,1)} %tri_sums.3), calls=%async_computation.4 | async-start | bytes 6291456 | tf_op jit(solution)/shard_map/all_to_all | solution.py:411
  271.3 93.2 %collective-permute-start.3 = (bf16[8,16,16,512]{3,2,1,0:T(8,128)(2,1)}, bf16[8,16,16,512]{3,2,1,0:T(8,128)(2,1)}, u32[]{:S(2)}, u32[]{:S(2)}) collective-permute-start(bf16[8,16,16,512]{3,2,1,0:T(8,128)(2,1)} %all-to-all-done.1.refs_1_), channel_id=1, source_target_pairs={{0,8},{1,9},{2,10},{3,11},{4,12},{5,13},{6,14},{7,15},{8,0},{9,1},... | collective-permute-start | bytes 6291464 | tf_op jit(solution)/shard_map/ppermute | solution.py:393
  369.7 7.5 %copy-start.8 = (s32[2,4]{1,0:T(2,128)S(1)}, s32[2,4]{1,0:T(2,128)}, u32[]{:S(2)}) copy-start(s32[2,4]{1,0:T(2,128)} %constant.103.clone) | copy-start | bytes 100
  369.7 7.5 %copy-start.9 = (s32[1,4]{1,0:T(1,128)S(1)}, s32[1,4]{1,0:T(1,128)}, u32[]{:S(2)}) copy-start(s32[1,4]{1,0:T(1,128)} %constant.105) | copy-start | bytes 52
  369.7 15.3 %copy-start = (bf16[8,16,32,384]{3,2,1,0:T(8,128)(2,1)}, bf16[8,16,32,384]{3,2,1,0:T(8,128)(2,1)S(1)}, u32[]{:S(2)}) copy-start(bf16[8,16,32,384]{3,2,1,0:T(8,128)(2,1)S(1)} %all-to-all-done.4) | copy-start | bytes 9437188
  369.7 76.5 %all-to-all-start.2 = ((bf16[8,16,32,128]{3,2,1,0:T(8,128)(2,1)}), bf16[8,16,32,128]{3,2,1,0:T(8,128)(2,1)}, u32[]{:S(2)}, u32[]{:S(2)}) async-start(bf16[8,16,32,128]{3,2,1,0:T(8,128)(2,1)} %tri_sums.2), calls=%async_computation.2 | async-start | bytes 2097152 | tf_op jit(solution)/shard_map/all_to_all | solution.py:411
  377.4 11.4 %copy-start.7 = (s32[2,4]{1,0:T(2,128)}, s32[2,4]{1,0:T(2,128)S(1)}, u32[]{:S(2)}) copy-start(s32[2,4]{1,0:T(2,128)S(1)} %scatter.4) | copy-start | bytes 100
Sparse Core Ops, SparseCore 0:
  95.4 77.3 all-gather.4
  258.4 74.6 all-gather.6
where the time goes:
time: 465 us; the launch traced here: 463 us
  waiting for transfers between devices  215 us (46%)
  Pallas kernels  170 us (37%)
  starting transfers between devices  40.7 us (9%)
  local copies, waits for them, and re-layouts  18.9 us (4%)
  between operations  14.2 us (3%)
    ppermute x2, waiting for transfers between devices, body(): right_oth.append(lax.ppermute(right_own[part], 'row', swap))  89.9 us
    all_gather x2, waiting for transfers between devices, gather(): values = lax.all_gather(values, 'row', axis=0, axis_index_groups=within)  67.8 us
    pallas_call x1, Pallas kernels, msa_block(): pl.pallas_call(functools.partial(msa_kernel, width, divisor(res, 256), or...  50.2 us
    ppermute x6, waiting for transfers between devices, across(): lax.ppermute(values[k], 'row', [(r, r ^ k * members) for r in range(ring)])  42.5 us
    pallas_call x1, Pallas kernels, opm_block(): pl.pallas_call(opm_kernel, grid=(owned // rows,), in_specs=[pl.BlockSpec(...  35.1 us
    pallas_call x2, Pallas kernels, pair_tail(): pl.pallas_call(tail_kernel, grid_spec=pltpu.PrefetchScalarGridSpec(num_sc...  32 us
    pallas_call x3, Pallas kernels, pair_head(): pl.pallas_call(head_kernel, grid=(steps,), in_specs=[pl.BlockSpec((rows,...  31.4 us
    all_to_all x3, starting transfers between devices, spread(): lax.all_to_all(values, 'row', 0, 0, tiled=True, axis_index_groups=halves)  17.4 us
  transfers between devices with their start and end apart: 15, of which 8 were waited for; matrix products, arithmetic and copies ran while one was open for 4% of the time, Pallas kernels for 33%

commit v1 on v0

--- a/solution.py
+++ b/solution.py
@@ -12,7 +12,7 @@
 F32 = jnp.float32
 BF16 = jnp.bfloat16
 LANES = 128
-HEAD_UNROLL = 4
+HEAD_UNROLL = 8
 TAIL_UNROLL = 2
 TAIL_ROWS = 8
 
@@ -389,10 +389,11 @@
     right_own, right_oth = [], []
     for part in range(parts):
         right = made[part]
+        if part:
+            right, bias = lax.optimization_barrier((right, bias))
         right_own.append(spread(right))
         right_oth.append(lax.ppermute(right_own[part], "row", swap))
     left = pair_head(coupling_features, my_residue, residue, trio[0 : 2 * cz])
-    left, bias = lax.optimization_barrier((left, bias))
     left_own = spread(left)
     bias_all = gather(bias)
 
@@ -421,13 +422,19 @@
     left_res = left_res.transpose(3, 0, 2, 1).reshape(owned, ring * seqs, outer)
     entry_order = entry.reshape(planes, members, seqs, res).transpose(1, 0, 2, 3).reshape(ring * seqs, res)
     mine = lax.dynamic_slice_in_dim(entry_order, place * owned, owned, 1)
-    opm = opm_block(left_res, both, product_final_matrix.reshape(outer, outer * cz), entry_order.T.astype(BF16), mine)
+    outer_map = product_final_matrix.reshape(outer, outer * cz)
+    gate_map = trio_factor_matrices[:, 4 * cz : 5 * cz]
+    entry_t = entry_order.T.astype(BF16)
+    left_own, left_res, outer_map, gate_map, entry_t, mine = lax.optimization_barrier(
+        (left_own, left_res, outer_map, gate_map, entry_t, mine)
+    )
+    opm = opm_block(left_res, both, outer_map, entry_t, mine)
 
     sums = tri_sums(left_own, right_own + right_oth[:-1])
     tri_near = collect(sums)
     sums = tri_sums(left_own, right_oth[-1:])
     tri_last = collect(sums)
-    weights = (trio_factor_matrices[:, 4 * cz : 5 * cz], trio_final_matrix, feedforward_expand, feedforward_shrink)
+    weights = (gate_map, trio_final_matrix, feedforward_expand, feedforward_shrink)
     table = jnp.array([[0] * parts + [1] * parts, list(range(parts)) * 2], jnp.int32)
     table = table.at[0].set(table[0] ^ half)
     pair = pair_tail(table[:, :-1], parts, coupling_features, tri_near, opm, weights)

time: 465 us -> 478 us (1.028)
  waiting for transfers between devices: 215 us -> 232 us
  local copies, waits for them, and re-layouts: 18.9 us -> 13.3 us
  starting transfers between devices: 40.7 us -> 46.1 us
    ppermute x2, waiting for transfers between devices: 89.9 us -> 121 us  [body(): right_oth.append(lax.ppermute(right_own[part], 'row', swap))]
    all_gather x2, waiting for transfers between devices: 67.8 us -> 53.5 us  [gather(): values = lax.all_gather(values, 'row', axis=0, axis_index_groups=within)]
    ppermute x6, waiting for transfers between devices: 42.5 us -> 36 us  [across(): lax.ppermute(values[k], 'row', [(r, r ^ k * members) for r in range(ring)])]
    all_to_all x3, waiting for transfers between devices: 15.1 us -> 21.3 us  [spread(): lax.all_to_all(values, 'row', 0, 0, tiled=True, axis_index_groups=halves)]
    ppermute x2, starting transfers between devices: 5.69 us -> 0.25 us  [body(): right_oth.append(lax.ppermute(right_own[part], 'row', swap))]
    all_to_all x3, starting transfers between devices: 17.4 us -> 22.8 us  [spread(): lax.all_to_all(values, 'row', 0, 0, tiled=True, axis_index_groups=halves)]
  transfers between devices with their start and end apart: 15 -> 15, of which waited for: 8 -> 9; matrix products, arithmetic and copies ran while one was open for 4% -> 3% of each run, Pallas kernels for 33% -> 30%
where the time goes in v1:
time: 478 us; the launch traced here: 476 us
  waiting for transfers between devices  232 us (49%)
  Pallas kernels  167 us (35%)
  starting transfers between devices  46.1 us (10%)
  between operations  14.2 us (3%)
  local copies, waits for them, and re-layouts  13.3 us (3%)
    ppermute x2, waiting for transfers between devices, body(): right_oth.append(lax.ppermute(right_own[part], 'row', swap))  121 us
    all_gather x2, waiting for transfers between devices, gather(): values = lax.all_gather(values, 'row', axis=0, axis_index_groups=within)  53.5 us
    pallas_call x1, Pallas kernels, msa_block(): pl.pallas_call(functools.partial(msa_kernel, width, divisor(res, 256), or...  50.2 us
    ppermute x6, waiting for transfers between devices, across(): lax.ppermute(values[k], 'row', [(r, r ^ k * members) for r in range(ring)])  36 us
    pallas_call x1, Pallas kernels, opm_block(): pl.pallas_call(opm_kernel, grid=(owned // rows,), in_specs=[pl.BlockSpec(...  35.1 us
    pallas_call x2, Pallas kernels, pair_tail(): pl.pallas_call(tail_kernel, grid_spec=pltpu.PrefetchScalarGridSpec(num_sc...  32 us
    pallas_call x3, Pallas kernels, pair_head(): pl.pallas_call(head_kernel, grid=(steps,), in_specs=[pl.BlockSpec((rows,...  29.4 us
    all_to_all x3, starting transfers between devices, spread(): lax.all_to_all(values, 'row', 0, 0, tiled=True, axis_index_groups=halves)  22.8 us
  transfers between devices with their start and end apart: 15, of which 9 were waited for; matrix products, arithmetic and copies ran while one was open for 3% of the time, Pallas kernels for 30%

profile of v1, /device:TPU:13, one launch (start us, length us, event | category | flops | bytes accessed | tf_op | source)
XLA Modules:
  0.0 475.8 jit_solution(7591416806101603555)
XLA Ops:
  7.2 7.8 %pair_bias.1 = bf16[8,32,512]{2,1,0:T(8,128)(2,1)} custom-call(bf16[32,512,128]{2,1,0:T(8,128)(2,1)} %x_ref.9, bf16[8,128]{1,0:T(8,128)(2,1)} %bitcast.74), custom_call_target="tpu_custom_call" | custom-call | tf_op jit(solution)/shard_map/pair_bias/pallas_call | solution.py:69
  15.1 1.3 collective-permute-start.2
  17.4 1.2 collective-permute-start
  20.2 8.1 %pair_head.3 = bf16[128,16,512]{2,1,0:T(8,128)(2,1)} custom-call(bf16[32,512,128]{2,1,0:T(8,128)(2,1)} %x_ref.9, f32[2,1,16]{2,1,0:T(1,128)} %bitcast.70, f32[1,512]{1,0:T(1,128)} %bitcast.66, bf16[256,128]{1,0:T(8,128)(2,1)} %get-tuple-element.53.w_ref), custom_call_target="tpu_custom_call" | custom-call | tf_op jit(solution)/shard_map/pair_head/pallas_call | solution.py:100
  28.3 5.6 %collective-permute-done.2 = bf16[8,32,512]{2,1,0:T(8,128)(2,1)S(1)} collective-permute-done((bf16[8,32,512]{2,1,0:T(8,128)(2,1)}, bf16[8,32,512]{2,1,0:T(8,128)(2,1)S(1)}, u32[]{:S(2)}, u32[]{:S(2)}) %collective-permute-start.2) | collective-permute-done | bytes 262176 | tf_op jit(solution)/shard_map/ppermute | solution.py:380
  33.9 4.6 collective-permute-done.1
  38.8 1.1 pad_maximum_fusion.3
  39.9 8.1 %pair_head.5 = bf16[128,16,512]{2,1,0:T(8,128)(2,1)} custom-call(bf16[32,512,128]{2,1,0:T(8,128)(2,1)} %x_ref.9, f32[2,1,16]{2,1,0:T(1,128)} %bitcast.71, f32[1,512]{1,0:T(1,128)} %bitcast.67, bf16[256,128]{1,0:T(8,128)(2,1)} %get-tuple-element.53.w_ref), custom_call_target="tpu_custom_call" | custom-call | tf_op jit(solution)/shard_map/pair_head/pallas_call | solution.py:100
  48.0 6.9 %all-to-all-start.3 = ((bf16[8,16,16,512]{3,2,1,0:T(8,128)(2,1)}), bf16[8,16,16,512]{3,2,1,0:T(8,128)(2,1)S(1)}, u32[]{:S(2)}, u32[]{:S(2)}) async-start(bf16[8,16,16,512]{3,2,1,0:T(8,128)(2,1)} %bitcast.50), calls=%async_computation.3 | async-start | bytes 4194304 | tf_op jit(solution)/shard_map/all_to_all | solution.py:362
  54.9 13.3 %pair_head.4 = bf16[128,32,512]{2,1,0:T(8,128)(2,1)} custom-call(bf16[32,512,128]{2,1,0:T(8,128)(2,1)} %x_ref.9, f32[2,1,16]{2,1,0:T(1,128)} %bitcast.72, f32[1,512]{1,0:T(1,128)} %bitcast.68, bf16[256,128]{1,0:T(8,128)(2,1)} %get-tuple-element.52.w_ref), custom_call_target="tpu_custom_call" | custom-call | tf_op jit(solution)/shard_map/pair_head/pallas_call | solution.py:100
  68.1 21.2 %all-to-all-done.3.refs_0_ = bf16[8,16,16,512]{3,2,1,0:T(8,128)(2,1)S(1)} async-done(((bf16[8,16,16,512]{3,2,1,0:T(8,128)(2,1)}), bf16[8,16,16,512]{3,2,1,0:T(8,128)(2,1)S(1)}, u32[]{:S(2)}, u32[]{:S(2)}) %all-to-all-start.3) | async-done | bytes 2097184 | tf_op jit(solution)/shard_map/all_to_all | solution.py:362
  89.4 7.4 %all-to-all-start = ((bf16[8,16,32,512]{3,2,1,0:T(8,128)(2,1)}), bf16[8,16,32,512]{3,2,1,0:T(8,128)(2,1)}, u32[]{:S(2)}, u32[]{:S(2)}) async-start(bf16[8,16,32,512]{3,2,1,0:T(8,128)(2,1)} %bitcast.47), calls=%async_computation | async-start | bytes 8388608 | tf_op jit(solution)/shard_map/all_to_all | solution.py:362
  97.4 1.7 all-gather.5.cloned.1.call-done.bias_ref
  99.1 50.2 %msa_block.1 = (bf16[8,512,256]{2,1,0:T(8,128)(2,1)}, bf16[8,32,512]{2,1,0:T(8,128)(2,1)}, bf16[8,32,512]{2,1,0:T(8,128)(2,1)}) custom-call(bf16[8,512,256]{2,1,0:T(8,128)(2,1)} %x_ref.7, f32[8,1,512]{2,1,0:T(1,128)} %reshape.88.valid_ref, bf16[16,8,32,512]{3,2,1,0:T(8,128)(2,1)} %all-gather.5.cloned.1.call-done.bias_ref, bf16[256,1024]{1,0:T(8,128)(2,1)} %w_ref.1, ...), custom_call_target="tpu_custom_call" | custom-call | tf_op jit(solution)/shard_map/msa_block/pallas_call | solution.py:163
  151.4 1.3 collective-permute-start.5
  152.7 1.1 collective-permute-start.4
  154.8 19.7 %collective-permute-done.5 = bf16[32,8,640]{2,0,1:T(8,128)(2,1)S(1)} collective-permute-done((bf16[32,8,640]{2,0,1:T(8,128)(2,1)S(1)}, bf16[32,8,640]{2,0,1:T(8,128)(2,1)S(1)}, u32[]{:S(2)}, u32[]{:S(2)}) %collective-permute-start.5) | collective-permute-done | bytes 327712 | tf_op jit(solution)/shard_map/ppermute | solution.py:380
  174.5 6.0 %collective-permute-done.4 = bf16[32,8,640]{2,0,1:T(8,128)(2,1)S(1)} collective-permute-done((bf16[32,8,640]{2,0,1:T(8,128)(2,1)S(1)}, bf16[32,8,640]{2,0,1:T(8,128)(2,1)S(1)}, u32[]{:S(2)}, u32[]{:S(2)}) %collective-permute-start.4) | collective-permute-done | bytes 327712 | tf_op jit(solution)/shard_map/ppermute | solution.py:380
  181.1 1.5 copy.66
  182.6 8.6 %all-to-all-start.1 = ((bf16[8,16,16,512]{3,2,1,0:T(8,128)(2,1)}), bf16[8,16,16,512]{3,2,1,0:T(8,128)(2,1)}, u32[]{:S(2)}, u32[]{:S(2)}) async-start(bf16[8,16,16,512]{3,2,1,0:T(8,128)(2,1)} %bitcast.25), calls=%async_computation.1 | async-start | bytes 4194304 | tf_op jit(solution)/shard_map/all_to_all | solution.py:362
  193.5 51.8 %all-gather.7.cloned.1.call-done.r_ref = bf16[16,32,8,640]{3,2,1,0:T(8,128)(2,1)} async-done(((bf16[4,32,8,640]{3,2,1,0:T(8,128)(2,1)}), bf16[16,32,8,640]{3,2,1,0:T(8,128)(2,1)}) %all-gather.7.cloned.1.call-update) | async-done | bytes 5242896 | tf_op jit(solution)/shard_map/all_gather | solution.py:385
  245.2 1.6 dynamic-slice_bitcast_fusion
  246.8 2.7 copy.67
  249.5 31.4 %collective-permute-done.7.refs_2_ = bf16[8,16,16,512]{3,2,1,0:T(8,128)(2,1)} collective-permute-done((bf16[8,16,16,512]{3,2,1,0:T(8,128)(2,1)S(1)}, bf16[8,16,16,512]{3,2,1,0:T(8,128)(2,1)}, u32[]{:S(2)}, u32[]{:S(2)}) %collective-permute-start.7) | collective-permute-done | bytes 2097184 | tf_op jit(solution)/shard_map/ppermute | solution.py:395
  280.9 7.7 %tri_sums.3 = bf16[8,16,32,384]{3,2,1,0:T(8,128)(2,1)} custom-call(bf16[8,16,32,512]{3,2,1,0:T(8,128)(2,1)} %all-to-all-done.l_ref, bf16[8,16,16,512]{3,2,1,0:T(8,128)(2,1)} %copy-done.1, bf16[8,16,16,512]{3,2,1,0:T(8,128)(2,1)} %all-to-all-done.1.refs_1_, bf16[8,16,16,512]{3,2,1,0:T(8,128)(2,1)} %collective-permute-done.7.refs_2_), custom_call_target="tpu_custom_call" | custom-call | tf_op jit(solution)/shard_map/tri_sums/pallas_call | solution.py:208
  288.6 7.9 %all-to-all-start.4 = ((bf16[8,16,32,384]{3,2,1,0:T(8,128)(2,1)}), bf16[8,16,32,384]{3,2,1,0:T(8,128)(2,1)S(1)}, u32[]{:S(2)}, u32[]{:S(2)}) async-start(bf16[8,16,32,384]{3,2,1,0:T(8,128)(2,1)} %tri_sums.3), calls=%async_computation.4 | async-start | bytes 6291456 | tf_op jit(solution)/shard_map/all_to_all | solution.py:412
  296.7 89.9 %collective-permute-done.6.refs_0_ = bf16[8,16,16,512]{3,2,1,0:T(8,128)(2,1)} collective-permute-done((bf16[8,16,16,512]{3,2,1,0:T(8,128)(2,1)}, bf16[8,16,16,512]{3,2,1,0:T(8,128)(2,1)}, u32[]{:S(2)}, u32[]{:S(2)}) %collective-permute-start.6) | collective-permute-done | bytes 2097184 | tf_op jit(solution)/shard_map/ppermute | solution.py:395
  386.6 5.1 %tri_sums.2 = bf16[8,16,32,128]{3,2,1,0:T(8,128)(2,1)} custom-call(bf16[8,16,32,512]{3,2,1,0:T(8,128)(2,1)} %all-to-all-done.l_ref, bf16[8,16,16,512]{3,2,1,0:T(8,128)(2,1)} %collective-permute-done.6.refs_0_), custom_call_target="tpu_custom_call" | custom-call | tf_op jit(solution)/shard_map/tri_sums/pallas_call | solution.py:208
  391.7 8.2 %all-to-all-start.2 = ((bf16[8,16,32,128]{3,2,1,0:T(8,128)(2,1)}), bf16[8,16,32,128]{3,2,1,0:T(8,128)(2,1)}, u32[]{:S(2)}, u32[]{:S(2)}) async-start(bf16[8,16,32,128]{3,2,1,0:T(8,128)(2,1)} %tri_sums.2), calls=%async_computation.2 | async-start | bytes 2097152 | tf_op jit(solution)/shard_map/all_to_all | solution.py:412
  401.8 35.1 %opm_block.1 = f32[32,512,128]{2,1,0:T(8,128)} custom-call(bf16[32,128,32]{2,1,0:T(8,128)(2,1)} %bitcast.51, bf16[16,32,8,640]{3,2,1,0:T(8,128)(2,1)} %all-gather.7.cloned.1.call-done.r_ref, bf16[32,4096]{1,0:T(8,128)(2,1)} %reshape.95.w_ref, bf16[512,128]{1,0:T(8,128)(2,1)} %bitcast.58, f32[4,128,8]{2,1,0:T(8,128)} %bitcast.56), custom_call_target="tpu_custom_call" | custom-call | tf_op jit(solution)/shard_map/opm_block/pallas_call | solution.py:255
  436.9 22.3 %pair_tail.2.refs_0_ = bf16[32,16,2,16,128]{4,3,2,1,0:T(8,128)(2,1)} custom-call(s32[2,3]{1,0:T(2,128)} %bitcast.73, bf16[32,16,2,16,128]{4,3,2,1,0:T(8,128)(2,1)} %bitcast.43, bf16[128,32,384]{2,1,0:T(8,128)(2,1)} %bitcast.49, f32[32,16,2,16,128]{4,3,2,1,0:T(8,128)} %bitcast.45, bf16[128,128]{1,0:T(8,128)(2,1)} %slice.38.wg_ref, bf16[128,128]{1,0:T(8,128)(2,1)} %wt_ref.3, ...), custom_call_target="tpu_custom_call" | custom-call | tf_op jit(solution)/shard_map/pair_tail/pallas_call | solution.py:311
  459.2 9.7 %pair_tail.3 = bf16[32,16,2,16,128]{4,3,2,1,0:T(8,128)(2,1)} custom-call(s32[2,1]{1,0:T(2,128)} %slice.36.table_ref, bf16[32,16,2,16,128]{4,3,2,1,0:T(8,128)(2,1)} %bitcast.44, bf16[128,32,128]{2,1,0:T(8,128)(2,1)} %bitcast.26.tri_ref, f32[32,16,2,16,128]{4,3,2,1,0:T(8,128)} %bitcast.46, ...), custom_call_target="tpu_custom_call", output_to_operand_aliasing={{}: (8, {})} | custom-call | tf_op jit(solution)/shard_map/pair_tail/pallas_call | solution.py:311
  (64 shorter events, 11.5 us)
Async XLA Ops:
  7.2 92.0 %all-gather.5.cloned.1.call-start = ((), (), s32[]{:S(2)}) async-start(), calls=%async_computation.5 | async-start | bytes 5242880 | tf_op jit(solution)/shard_map/all_gather | solution.py:385
  7.2 11.3 %copy-start.9 = (s32[512]{0:T(512)S(1)}, s32[512]{0:T(512)}, u32[]{:S(2)}) copy-start(s32[512]{0:T(512)} %param.19) | copy-start | bytes 6148
  7.2 12.1 %copy-start.5 = (bf16[128,640]{1,0:T(8,128)(2,1)S(1)}, bf16[128,640]{1,0:T(8,128)(2,1)}, u32[]{:S(2)}) copy-start(bf16[128,640]{1,0:T(8,128)(2,1)} %param.25) | copy-start | bytes 491524
  15.1 18.8 %collective-permute-start.2 = (bf16[8,32,512]{2,1,0:T(8,128)(2,1)}, bf16[8,32,512]{2,1,0:T(8,128)(2,1)S(1)}, u32[]{:S(2)}, u32[]{:S(2)}) collective-permute-start(bf16[8,32,512]{2,1,0:T(8,128)(2,1)} %pair_bias.1), channel_id=1, source_target_pairs={{0,12},{1,13},{2,14},{3,15},{4,8},{5,9},{6,10},{7,11},{8,4},{9,5},... | collective-permute-start | bytes 786440 | tf_op jit(solution)/shard_map/ppermute | solution.py:380
  16.4 22.2 %collective-permute-start.1 = (bf16[8,32,512]{2,1,0:T(8,128)(2,1)}, bf16[8,32,512]{2,1,0:T(8,128)(2,1)S(1)}, u32[]{:S(2)}, u32[]{:S(2)}) collective-permute-start(bf16[8,32,512]{2,1,0:T(8,128)(2,1)} %pair_bias.1), channel_id=1, source_target_pairs={{0,8},{1,9},{2,10},{3,11},{4,12},{5,13},{6,14},{7,15},{8,0},{9,1},... | collective-permute-start | bytes 786440 | tf_op jit(solution)/shard_map/ppermute | solution.py:380
  17.4 21.1 %collective-permute-start = (bf16[8,32,512]{2,1,0:T(8,128)(2,1)}, bf16[8,32,512]{2,1,0:T(8,128)(2,1)S(1)}, u32[]{:S(2)}, u32[]{:S(2)}) collective-permute-start(bf16[8,32,512]{2,1,0:T(8,128)(2,1)} %pair_bias.1), channel_id=1, source_target_pairs={{0,4},{1,5},{2,6},{3,7},{4,0},{5,1},{6,2},{7,3},{8,12},{9,13},{10,... | collective-permute-start | bytes 786440 | tf_op jit(solution)/shard_map/ppermute | solution.py:380
  18.6 1.6 copy-start.6
  20.1 18.4 %copy-start.2 = (bf16[8,32,512]{2,1,0:T(8,128)(2,1)S(1)}, bf16[8,32,512]{2,1,0:T(8,128)(2,1)}, u32[]{:S(2)}) copy-start(bf16[8,32,512]{2,1,0:T(8,128)(2,1)} %pair_bias.1) | copy-start | bytes 786436
  48.0 41.4 %all-to-all-start.3 = ((bf16[8,16,16,512]{3,2,1,0:T(8,128)(2,1)}), bf16[8,16,16,512]{3,2,1,0:T(8,128)(2,1)S(1)}, u32[]{:S(2)}, u32[]{:S(2)}) async-start(bf16[8,16,16,512]{3,2,1,0:T(8,128)(2,1)} %bitcast.50), calls=%async_computation.3 | async-start | bytes 4194304 | tf_op jit(solution)/shard_map/all_to_all | solution.py:362
  89.4 101.8 %copy-start.1 = (bf16[8,16,16,512]{3,2,1,0:T(8,128)(2,1)}, bf16[8,16,16,512]{3,2,1,0:T(8,128)(2,1)S(1)}, u32[]{:S(2)}) copy-start(bf16[8,16,16,512]{3,2,1,0:T(8,128)(2,1)S(1)} %all-to-all-done.3.refs_0_) | copy-start | bytes 6291460
  89.4 7.4 %copy-start.3 = (s32[128,512]{1,0:T(8,128)S(1)}, s32[128,512]{1,0:T(8,128)}, u32[]{:S(2)}) copy-start(s32[128,512]{1,0:T(8,128)} %param.18) | copy-start | bytes 786436
  89.4 7.4 %copy-start.7 = (f32[512]{0:T(512)S(1)}, f32[512]{0:T(512)}, u32[]{:S(2)}) copy-start(f32[512]{0:T(512)} %copy-done.6) | copy-start | bytes 6148
  89.4 93.2 %all-to-all-start = ((bf16[8,16,32,512]{3,2,1,0:T(8,128)(2,1)}), bf16[8,16,32,512]{3,2,1,0:T(8,128)(2,1)}, u32[]{:S(2)}, u32[]{:S(2)}) async-start(bf16[8,16,32,512]{3,2,1,0:T(8,128)(2,1)} %bitcast.47), calls=%async_computation | async-start | bytes 8388608 | tf_op jit(solution)/shard_map/all_to_all | solution.py:362
  96.8 148.5 %all-gather.7.cloned.1.call-start = ((), (), s32[]{:S(2)}) async-start(), calls=%async_computation.6 | async-start | bytes 6553600 | tf_op jit(solution)/shard_map/all_gather | solution.py:385
  151.4 23.1 %collective-permute-start.5 = (bf16[32,8,640]{2,0,1:T(8,128)(2,1)S(1)}, bf16[32,8,640]{2,0,1:T(8,128)(2,1)S(1)}, u32[]{:S(2)}, u32[]{:S(2)}) collective-permute-start(bf16[32,8,640]{2,0,1:T(8,128)(2,1)S(1)} %get-tuple-element.47), channel_id=1, source_target_pairs={{0,12},{1,13},{2,14},{3,15},{4,8},{5,9},{6,10},{7,11},{8,4},{9,5},... | collective-permute-start | bytes 983048 | tf_op jit(solution)/shard_map/ppermute | solution.py:380
  152.7 27.8 %collective-permute-start.4 = (bf16[32,8,640]{2,0,1:T(8,128)(2,1)S(1)}, bf16[32,8,640]{2,0,1:T(8,128)(2,1)S(1)}, u32[]{:S(2)}, u32[]{:S(2)}) collective-permute-start(bf16[32,8,640]{2,0,1:T(8,128)(2,1)S(1)} %get-tuple-element.46), channel_id=1, source_target_pairs={{0,8},{1,9},{2,10},{3,11},{4,12},{5,13},{6,14},{7,15},{8,0},{9,1},... | collective-permute-start | bytes 983048 | tf_op jit(solution)/shard_map/ppermute | solution.py:380
  153.8 26.7 %collective-permute-start.3 = (bf16[32,8,640]{2,0,1:T(8,128)(2,1)S(1)}, bf16[32,8,640]{2,0,1:T(8,128)(2,1)S(1)}, u32[]{:S(2)}, u32[]{:S(2)}) collective-permute-start(bf16[32,8,640]{2,0,1:T(8,128)(2,1)S(1)} %get-tuple-element.45), channel_id=1, source_target_pairs={{0,4},{1,5},{2,6},{3,7},{4,0},{5,1},{6,2},{7,3},{8,12},{9,13},{10,... | collective-permute-start | bytes 983048 | tf_op jit(solution)/shard_map/ppermute | solution.py:380
  182.6 9.2 %copy-start.4 = (bf16[1024,128]{1,0:T(8,128)(2,1)S(1)}, bf16[1024,128]{1,0:T(8,128)(2,1)}, u32[]{:S(2)}) copy-start(bf16[1024,128]{1,0:T(8,128)(2,1)} %param.24) | copy-start | bytes 786436
  182.6 66.9 %all-to-all-start.1 = ((bf16[8,16,16,512]{3,2,1,0:T(8,128)(2,1)}), bf16[8,16,16,512]{3,2,1,0:T(8,128)(2,1)}, u32[]{:S(2)}, u32[]{:S(2)}) async-start(bf16[8,16,16,512]{3,2,1,0:T(8,128)(2,1)} %bitcast.25), calls=%async_computation.1 | async-start | bytes 4194304 | tf_op jit(solution)/shard_map/all_to_all | solution.py:362
  191.1 89.7 %collective-permute-start.7 = (bf16[8,16,16,512]{3,2,1,0:T(8,128)(2,1)S(1)}, bf16[8,16,16,512]{3,2,1,0:T(8,128)(2,1)}, u32[]{:S(2)}, u32[]{:S(2)}) collective-permute-start(bf16[8,16,16,512]{3,2,1,0:T(8,128)(2,1)S(1)} %all-to-all-done.3.refs_0_), channel_id=1, source_target_pairs={{0,8},{1,9},{2,10},{3,11},{4,12},{5,13},{6,14},{7,15},{8,0},{9,1},... | collective-permute-start | bytes 6291464 | tf_op jit(solution)/shard_map/ppermute | solution.py:395
  288.6 103.1 %all-to-all-start.4 = ((bf16[8,16,32,384]{3,2,1,0:T(8,128)(2,1)}), bf16[8,16,32,384]{3,2,1,0:T(8,128)(2,1)S(1)}, u32[]{:S(2)}, u32[]{:S(2)}) async-start(bf16[8,16,32,384]{3,2,1,0:T(8,128)(2,1)} %tri_sums.3), calls=%async_computation.4 | async-start | bytes 6291456 | tf_op jit(solution)/shard_map/all_to_all | solution.py:412
  296.5 90.2 %collective-permute-start.6 = (bf16[8,16,16,512]{3,2,1,0:T(8,128)(2,1)}, bf16[8,16,16,512]{3,2,1,0:T(8,128)(2,1)}, u32[]{:S(2)}, u32[]{:S(2)}) collective-permute-start(bf16[8,16,16,512]{3,2,1,0:T(8,128)(2,1)} %all-to-all-done.1.refs_1_), channel_id=1, source_target_pairs={{0,8},{1,9},{2,10},{3,11},{4,12},{5,13},{6,14},{7,15},{8,0},{9,1},... | collective-permute-start | bytes 6291464 | tf_op jit(solution)/shard_map/ppermute | solution.py:395
  391.7 8.3 %copy-start.10 = (s32[2,4]{1,0:T(2,128)S(1)}, s32[2,4]{1,0:T(2,128)}, u32[]{:S(2)}) copy-start(s32[2,4]{1,0:T(2,128)} %constant.103.clone) | copy-start | bytes 100
  391.7 8.3 %copy-start.11 = (s32[1,4]{1,0:T(1,128)S(1)}, s32[1,4]{1,0:T(1,128)}, u32[]{:S(2)}) copy-start(s32[1,4]{1,0:T(1,128)} %constant.105) | copy-start | bytes 52
  391.7 45.2 %copy-start = (bf16[8,16,32,384]{3,2,1,0:T(8,128)(2,1)}, bf16[8,16,32,384]{3,2,1,0:T(8,128)(2,1)S(1)}, u32[]{:S(2)}) copy-start(bf16[8,16,32,384]{3,2,1,0:T(8,128)(2,1)S(1)} %all-to-all-done.4) | copy-start | bytes 9437188
  391.7 67.5 %all-to-all-start.2 = ((bf16[8,16,32,128]{3,2,1,0:T(8,128)(2,1)}), bf16[8,16,32,128]{3,2,1,0:T(8,128)(2,1)}, u32[]{:S(2)}, u32[]{:S(2)}) async-start(bf16[8,16,32,128]{3,2,1,0:T(8,128)(2,1)} %tri_sums.2), calls=%async_computation.2 | async-start | bytes 2097152 | tf_op jit(solution)/shard_map/all_to_all | solution.py:412
  400.2 36.6 %copy-start.8 = (s32[2,4]{1,0:T(2,128)}, s32[2,4]{1,0:T(2,128)S(1)}, u32[]{:S(2)}) copy-start(s32[2,4]{1,0:T(2,128)S(1)} %scatter.4) | copy-start | bytes 100
Sparse Core Ops, SparseCore 0:
  40.0 59.0 all-gather.4
  182.7 62.4 all-gather.6
